TPU v7x, 512 devices: a whole 4x4x16 slice. The times are simulated.
512 devices in a mesh: dp: 16 (over z_hi, y), feat: 32 (over x, z_lo, core).
Axes of the slice: x: 4, y: 4, z: 16 (z_hi: 4, z_lo: 4; z = z_hi * 4 + z_lo), core: 2. Of those that a mesh axis runs over, the one named last changes fastest.
Arguments:
- sample: bfloat16 [16384, 2048], P(('dp', 'feat')), may hold values from -1800 to 1800
- pool: bfloat16 [32768, 2048], P(('dp', 'feat')), may hold values from -720 to 720
- old_min: float32 [32768], P(('dp', 'feat')), may hold values from 0.5 to 1.5
- centers: int32 [256], replicated, may hold values from 0 to 32767
Outputs:
- new_min: float32 [32768], P(('dp', 'feat'))
All inputs are finite; a program needn't handle non-finite values.
Results may differ from a plain program's by a relative error of at most 0.00045.
Values may be sent and summed in bfloat16 or wider, within the bound.
A program may use at most 64 MiB of HBM per device.

v0:
```python
import jax
import jax.numpy as jnp
from jax import lax
from jax.sharding import PartitionSpec as P

EPSILON = 1e-06
HIGHEST = lax.Precision.HIGHEST


def contract_rows(left_part, right_part):
    return lax.dot_general(
        left_part, right_part, (((0,), (0,)), ((), ())), preferred_element_type=jnp.float32
    )


def squared_terms(row_values, centre_rows):
    row_wide = row_values.astype(jnp.float32)
    centre_wide = centre_rows.astype(jnp.float32)
    row_norms = jnp.sum(row_wide * row_wide, axis=1)
    centre_norms = jnp.sum(centre_wide * centre_wide, axis=1)
    inner_products = lax.dot_general(
        row_values, centre_rows, (((1,), (1,)), ((), ())), preferred_element_type=jnp.float32
    )
    return row_norms[:, None] + centre_norms[None, :] - 2.0 * inner_products


def pick_rows(source, centers, offset):
    row_count = source.shape[0]
    local_index = centers - offset
    inside = (local_index >= 0) & (local_index < row_count)
    taken_rows = source[jnp.clip(local_index, 0, row_count - 1)].astype(jnp.float32)
    return jnp.where(inside[:, None], taken_rows, 0.0)


def per_device(sample, pool, old_min, centers):
    model_width = sample.shape[1]
    feat_count = lax.axis_size("feat")
    group_count = lax.axis_size("dp")
    row_block = model_width // feat_count
    col_block = model_width // group_count
    feat_index = lax.axis_index("feat")
    group_index = lax.axis_index("dp")
    row_start = feat_index * row_block
    col_start = group_index * col_block
    pool_count = pool.shape[0]
    sample_total = sample.shape[0] * feat_count * group_count
    row_offset = (group_index * feat_count + feat_index) * pool_count
    sample_wide = sample.astype(jnp.float32)
    own_squares = jnp.sum(sample_wide * sample_wide, axis=0)
    col_squares = lax.psum(own_squares, ("dp", "feat"))
    inverse = 1.0 / jnp.sqrt(col_squares / sample_total + EPSILON)
    portion = lax.all_gather(sample, "feat", axis=0, tiled=True)
    left_part = lax.dynamic_slice_in_dim(portion, row_start, row_block, 1)
    gram_part = contract_rows(left_part, portion)
    gram_part = gram_part / sample_total
    inverse_rows = lax.dynamic_slice_in_dim(inverse, row_start, row_block)
    inverse_cols = lax.dynamic_slice_in_dim(inverse, col_start, col_block)
    cov_block = lax.psum_scatter(gram_part, "dp", scatter_dimension=1, tiled=True)
    corr_block = inverse_rows[:, None] * cov_block * inverse_cols[None, :]
    corr_rows = lax.all_gather(corr_block, "dp", axis=1, tiled=True)
    corr_cols = lax.all_gather(corr_block, "feat", axis=0, tiled=True)
    rows_global = row_start + jnp.arange(row_block, dtype=jnp.int32)
    cols_global = col_start + jnp.arange(col_block, dtype=jnp.int32)
    all_index = jnp.arange(model_width, dtype=jnp.int32)
    eye_rows = (rows_global[:, None] == all_index[None, :]).astype(jnp.float32)
    eye_cols = (all_index[:, None] == cols_global[None, :]).astype(jnp.float32)
    eye_block = (rows_global[:, None] == cols_global[None, :]).astype(jnp.float32)
    first_rows = 0.5 * (3.0 * eye_rows - corr_rows)
    first_cols = 0.5 * (3.0 * eye_cols - corr_cols)
    updated_y = jnp.dot(corr_rows, first_cols, precision=HIGHEST)
    left_part = first_rows
    middle = jnp.dot(
        left_part, lax.all_gather(updated_y, "feat", axis=0, tiled=True), precision=HIGHEST
    )
    second_factor = 0.5 * (3.0 * eye_block - middle)
    root_block = jnp.dot(
        lax.all_gather(second_factor, "dp", axis=1, tiled=True), first_cols, precision=HIGHEST
    )
    weight_block = (inverse_rows[:, None] * root_block).astype(jnp.bfloat16)
    weight_cols = lax.all_gather(weight_block, "feat", axis=0, tiled=True)
    everything = jnp.dot(
        pool,
        lax.all_gather(weight_cols, "dp", axis=1, tiled=True),
        preferred_element_type=jnp.float32,
    ).astype(jnp.bfloat16)
    contribution = pick_rows(everything, centers, row_offset)
    centre_full = lax.psum(contribution, ("dp", "feat")).astype(jnp.bfloat16)
    squared = squared_terms(everything, centre_full)
    nearest = jnp.min(jnp.maximum(squared, 0.0), axis=1) / (2.0 * model_width)
    return jnp.minimum(old_min, nearest)


def solution(mesh):
    return jax.shard_map(
        per_device,
        mesh=mesh,
        in_specs=(P(("dp", "feat"), None), P(("dp", "feat"), None), P(("dp", "feat")), P()),
        out_specs=P(("dp", "feat")),
        check_vma=False,
    )
```

profile of v0, /device:TPU:1, one launch (start us, length us, event | category | flops | bytes accessed | tf_op | source)
XLA Modules:
  0.0 781.0 jit_solution(9917778738509852095)
XLA Ops:
  6.5 0.7 all-gather.5.cloned.1.call-update
  7.3 76.0 %all-gather.5.cloned.1.call-done = bf16[1024,2048]{1,0:T(8,128)(2,1)} async-done(((bf16[32,2048]{1,0:T(8,128)(2,1)}), bf16[1024,2048]{1,0:T(8,128)(2,1)}) %all-gather.5.cloned.1.call-update) | async-done | bytes 4194320 | tf_op jit(solution)/shard_map/all_gather | solution.py:52
  83.3 4.0 convolution_multiply_fusion
  87.5 105.5 %psum.14 = f32[2048]{0:T(1024)S(1)} all-reduce(f32[2048]{0:T(1024)S(1)} %multiply_reduce_fusion.2), channel_id=1, replica_groups=mesh['dp'=16,'feat'=32] {'dp','feat'}, use_global_device_ids=true, to_apply=%region_1.0 | all-reduce | flops 2048 | bytes 16384 | tf_op jit(solution)/shard_map/psum | solution.py:50
  193.0 0.1 dynamic_slice.9
  193.1 0.1 dynamic_slice.11
  193.2 3.6 reduce-scatter.2.cloned.1.call-done
  196.7 1.4 multiply_multiply_fusion
  198.2 51.9 %all_gather.22 = f32[64,2048]{1,0:T(8,128)S(1)} all-gather(f32[64,128]{1,0:T(8,128)} %multiply_multiply_fusion), channel_id=1, replica_groups=mesh['dp'=16,'feat'=32] {'dp'}, dimensions={1}, use_global_device_ids=true | all-gather | bytes 557056 | tf_op jit(solution)/shard_map/all_gather | solution.py:60
  250.2 11.2 %all-gather.7.cloned.1.call-done = f32[2048,128]{1,0:T(8,128)} async-done(((f32[64,128]{1,0:T(8,128)}), f32[2048,128]{1,0:T(8,128)}) %all-gather.7.cloned.1.call-update) | async-done | bytes 1048592 | tf_op jit(solution)/shard_map/all_gather | solution.py:61
  261.4 2.7 fusion.5
  264.2 62.7 %all-gather.9.cloned.1.call-done = f32[2048,128]{1,0:T(8,128)} async-done(((f32[64,128]{1,0:T(8,128)}), f32[2048,128]{1,0:T(8,128)}) %all-gather.9.cloned.1.call-update) | async-done | bytes 1048592 | tf_op jit(solution)/shard_map/all_gather | solution.py:73
  327.0 2.1 fusion.3
  329.1 50.6 %all_gather.25 = f32[64,2048]{1,0:T(8,128)S(1)} all-gather(f32[64,128]{1,0:T(8,128)S(1)} %fusion.3), channel_id=1, replica_groups=mesh['dp'=16,'feat'=32] {'dp'}, dimensions={1}, use_global_device_ids=true | all-gather | bytes 557056 | tf_op jit(solution)/shard_map/all_gather | solution.py:77
  379.7 2.1 fusion.4
  381.9 54.6 %all_gather.26 = bf16[2048,128]{1,0:T(8,128)(2,1)} all-gather(bf16[64,128]{1,0:T(8,128)(2,1)S(1)} %fusion.4), channel_id=1, replica_groups=mesh['dp'=16,'feat'=32] {'feat'}, dimensions={0}, use_global_device_ids=true | all-gather | bytes 540672 | tf_op jit(solution)/shard_map/all_gather | solution.py:80
  436.6 220.7 %all-gather.11.cloned.1.call-done = bf16[2048,2048]{1,0:T(8,128)(2,1)} async-done(((bf16[2048,128]{1,0:T(8,128)(2,1)}), bf16[2048,2048]{1,0:T(8,128)(2,1)}) %all-gather.11.cloned.1.call-update) | async-done | bytes 8388624 | tf_op jit(solution)/shard_map/all_gather | solution.py:83
  657.3 5.1 multiply_reduce_fusion.1
  662.3 1.4 gather_fusion
  663.7 1.6 convert_select_fusion
  665.3 107.9 %all-reduce.1 = bf16[256,2048]{1,0:T(8,128)(2,1)S(1)} all-reduce(f32[256,2048]{1,0:T(8,128)} %convert_select_fusion), channel_id=1, replica_groups=mesh['dp'=16,'feat'=32] {'dp','feat'}, use_global_device_ids=true, to_apply=%region_4.5 | all-reduce | flops 524288 | bytes 3145728 | tf_op jit(solution)/shard_map/psum | solution.py:87
  773.2 0.3 multiply_reduce_fusion
  773.4 0.5 fusion.2
  774.0 0.5 multiply_minimum_fusion
  (24 shorter events, 0.3 us)
Async XLA Ops:
  6.5 650.7 %copy-start = (bf16[64,2048]{1,0:T(8,128)(2,1)S(1)}, bf16[64,2048]{1,0:T(8,128)(2,1)}, u32[]{:S(2)}) copy-start(bf16[64,2048]{1,0:T(8,128)(2,1)} %param.5) | copy-start | bytes 786436
  6.5 80.9 %copy-start.1 = (bf16[32,2048]{1,0:T(8,128)(2,1)S(1)}, bf16[32,2048]{1,0:T(8,128)(2,1)}, u32[]{:S(2)}) copy-start(bf16[32,2048]{1,0:T(8,128)(2,1)} %param.4) | copy-start | bytes 393220
  6.5 76.8 %all-gather.5.cloned.1.call-start = ((), (), s32[]{:S(2)}) async-start(), calls=%async_computation.1 | async-start | bytes 4325376 | tf_op jit(solution)/shard_map/all_gather | solution.py:52
  7.3 189.5 %reduce-scatter.2.cloned.1.call-start = ((), (), s32[]{:S(2)}) async-start(), calls=%async_computation.2 | async-start | bytes 557056 | tf_op jit(solution)/shard_map/reduce_scatter | solution.py:58
  87.4 349.2 %copy-start.2 = (s32[256]{0:T(256)S(1)}, s32[256]{0:T(256)}, u32[]{:S(2)}) copy-start(s32[256]{0:T(256)} %param.7) | copy-start | bytes 3076
  87.4 174.0 %all-gather.7.cloned.1.call-start = ((), (), s32[]{:S(2)}) async-start(), calls=%async_computation.3 | async-start | bytes 1081344 | tf_op jit(solution)/shard_map/all_gather | solution.py:61
  198.2 128.8 %all-gather.9.cloned.1.call-start = ((), (), s32[]{:S(2)}) async-start(), calls=%async_computation.4 | async-start | bytes 1081344 | tf_op jit(solution)/shard_map/all_gather | solution.py:73
  264.2 393.1 %all-gather.11.cloned.1.call-start = ((), (), s32[]{:S(2)}) async-start(), calls=%async_computation.5 | async-start | bytes 8912896 | tf_op jit(solution)/shard_map/all_gather | solution.py:83
  663.7 110.3 %copy-start.3 = (f32[64]{0:T(128)S(1)}, f32[64]{0:T(128)}, u32[]{:S(2)}) copy-start(f32[64]{0:T(128)} %param.6) | copy-start | bytes 772
Sparse Core Ops, SparseCore 0:
  9.5 73.7 all-gather.4
  87.5 109.1 reduce-scatter.1
  199.1 62.2 all-gather.6
  264.3 62.6 all-gather.8
  436.6 220.5 all-gather.10
where the time goes:
time: 782 us; the launch traced here: 781 us
  waiting for transfers between devices  375 us (48%)
  blocking collectives  371 us (47%)
  matrix products  16.6 us (2%)
  between operations  13.3 us (2%)
    all_gather x1, waiting for transfers between devices, per_device(): lax.all_gather(weight_cols, 'dp', axis=1, tiled=True)  221 us
    psum x1, blocking collectives, per_device(): centre_full = lax.psum(contribution, ('dp', 'feat')).astype(jnp.bfloat16)  108 us
    psum x1, blocking collectives, per_device(): col_squares = lax.psum(own_squares, ('dp', 'feat'))  105 us
    all_gather x1, waiting for transfers between devices, per_device(): portion = lax.all_gather(sample, 'feat', axis=0, tiled=True)  76 us
    all_gather x1, waiting for transfers between devices, per_device(): lax.all_gather(updated_y, 'feat', axis=0, tiled=True)  62.7 us
    all_gather x1, blocking collectives, per_device(): weight_cols = lax.all_gather(weight_block, 'feat', axis=0, tiled=True)  54.6 us
    all_gather x1, blocking collectives, per_device(): corr_rows = lax.all_gather(corr_block, 'dp', axis=1, tiled=True)  51.9 us
    all_gather x1, blocking collectives, per_device(): lax.all_gather(second_factor, 'dp', axis=1, tiled=True)  50.6 us
  transfers between devices with their start and end apart: 5, of which 5 were waited for; matrix products, arithmetic and copies ran while one was open for 0% of the time, Pallas kernels for 0%

commit v1 on v0

--- a/solution.py
+++ b/solution.py
@@ -5,6 +5,11 @@
 
 EPSILON = 1e-06
 HIGHEST = lax.Precision.HIGHEST
+
+
+def summed_here(x, name):
+    terms = lax.all_gather(x, name)
+    return jnp.sum(terms, axis=0)
 
 
 def contract_rows(left_part, right_part):
@@ -47,7 +52,7 @@
     row_offset = (group_index * feat_count + feat_index) * pool_count
     sample_wide = sample.astype(jnp.float32)
     own_squares = jnp.sum(sample_wide * sample_wide, axis=0)
-    col_squares = lax.psum(own_squares, ("dp", "feat"))
+    col_squares = summed_here(own_squares, ("dp", "feat"))
     inverse = 1.0 / jnp.sqrt(col_squares / sample_total + EPSILON)
     portion = lax.all_gather(sample, "feat", axis=0, tiled=True)
     left_part = lax.dynamic_slice_in_dim(portion, row_start, row_block, 1)

time: 782 us -> 1590 us (2.03)
  waiting for transfers between devices: 375 us -> 1280 us
  blocking collectives: 371 us -> 263 us
    all_gather x0 -> x1, waiting for transfers between devices: none -> 803 us  [summed_here(): terms = lax.all_gather(x, name)]
    psum x1 -> x0, blocking collectives: 105 us -> none  [per_device(): col_squares = lax.psum(own_squares, ('dp', 'feat'))]
    reduce_scatter x1, waiting for transfers between devices: 3.57 us -> 107 us  [per_device(): lax.psum_scatter(gram_part, 'dp', scatter_dimension=1, tiled=True)]
  transfers between devices with their start and end apart: 5 -> 6, of which waited for: 5 -> 6; matrix products, arithmetic and copies ran while one was open for 0% -> 1% of each run, Pallas kernels for 0% -> 0%
where the time goes in v1:
time: 1590 us
  waiting for transfers between devices  1280 us (81%)
  blocking collectives  263 us (17%)
  matrix products  16.7 us (1%)
    all_gather x1, waiting for transfers between devices, summed_here(): terms = lax.all_gather(x, name)  803 us
    all_gather x1, waiting for transfers between devices, per_device(): lax.all_gather(weight_cols, 'dp', axis=1, tiled=True)  223 us
    psum x1, blocking collectives, per_device(): centre_full = lax.psum(contribution, ('dp', 'feat')).astype(jnp.bfloat16)  108 us
    reduce_scatter x1, waiting for transfers between devices, per_device(): lax.psum_scatter(gram_part, 'dp', scatter_dimension=1, tiled=True)  107 us
    all_gather x1, waiting for transfers between devices, per_device(): portion = lax.all_gather(sample, 'feat', axis=0, tiled=True)  74.4 us
    all_gather x1, waiting for transfers between devices, per_device(): lax.all_gather(updated_y, 'feat', axis=0, tiled=True)  62.5 us
    all_gather x1, blocking collectives, per_device(): weight_cols = lax.all_gather(weight_block, 'feat', axis=0, tiled=True)  52.7 us
    all_gather x1, blocking collectives, per_device(): corr_rows = lax.all_gather(corr_block, 'dp', axis=1, tiled=True)  51.7 us
  transfers between devices with their start and end apart: 6, of which 6 were waited for; matrix products, arithmetic and copies ran while one was open for 1% of the time, Pallas kernels for 0%

profile of v1, /device:TPU:1, one launch (start us, length us, event | category | flops | bytes accessed | tf_op | source)
XLA Modules:
  0.0 1589.4 jit_solution(2997330600667834882)
XLA Ops:
  6.5 0.7 all-gather.7.cloned.1.call-update
  7.3 1.5 multiply_reduce_fusion.2
  8.9 74.4 %all-gather.7.cloned.1.call-done = bf16[1024,2048]{1,0:T(8,128)(2,1)} async-done(((bf16[32,2048]{1,0:T(8,128)(2,1)}), bf16[1024,2048]{1,0:T(8,128)(2,1)}) %all-gather.7.cloned.1.call-update) | async-done | bytes 4194320 | tf_op jit(solution)/shard_map/all_gather | solution.py:57
  83.3 4.1 convolution_multiply_fusion
  87.5 802.9 %all-gather.15.cloned.1.call-done = f32[1048576]{0:T(1024)} async-done(((f32[2048]{0:T(1024)}), f32[1048576]{0:T(1024)}) %all-gather.15.cloned.1.call-update) | async-done | bytes 4194320 | tf_op jit(solution)/shard_map/all_gather | solution.py:11
  890.4 4.9 reshape.21
  895.3 2.4 reduce_sum.37
  897.9 107.3 %reduce-scatter.2.cloned.1.call-done = f32[64,128]{1,0:T(8,128)} async-done(((f32[64,2048]{1,0:T(8,128)}), f32[64,128]{1,0:T(8,128)}) %reduce-scatter.2.cloned.1.call-update) | async-done | bytes 32784 | tf_op jit(solution)/shard_map/reduce_scatter | solution.py:63
  1005.2 1.4 multiply_multiply_fusion
  1006.7 51.7 %all_gather.30 = f32[64,2048]{1,0:T(8,128)S(1)} all-gather(f32[64,128]{1,0:T(8,128)} %multiply_multiply_fusion), channel_id=1, replica_groups=mesh['dp'=16,'feat'=32] {'dp'}, dimensions={1}, use_global_device_ids=true | all-gather | bytes 557056 | tf_op jit(solution)/shard_map/all_gather | solution.py:65
  1058.4 11.0 all-gather.9.cloned.1.call-done
  1069.5 2.7 fusion.5
  1072.3 62.5 %all-gather.11.cloned.1.call-done = f32[2048,128]{1,0:T(8,128)} async-done(((f32[64,128]{1,0:T(8,128)}), f32[2048,128]{1,0:T(8,128)}) %all-gather.11.cloned.1.call-update) | async-done | bytes 1048592 | tf_op jit(solution)/shard_map/all_gather | solution.py:78
  1134.8 2.1 fusion.3
  1136.9 50.9 %all_gather.33 = f32[64,2048]{1,0:T(8,128)S(1)} all-gather(f32[64,128]{1,0:T(8,128)S(1)} %fusion.3), channel_id=1, replica_groups=mesh['dp'=16,'feat'=32] {'dp'}, dimensions={1}, use_global_device_ids=true | all-gather | bytes 557056 | tf_op jit(solution)/shard_map/all_gather | solution.py:82
  1187.8 2.1 fusion.4
  1189.9 52.7 %all_gather.34 = bf16[2048,128]{1,0:T(8,128)(2,1)} all-gather(bf16[64,128]{1,0:T(8,128)(2,1)S(1)} %fusion.4), channel_id=1, replica_groups=mesh['dp'=16,'feat'=32] {'feat'}, dimensions={0}, use_global_device_ids=true | all-gather | bytes 540672 | tf_op jit(solution)/shard_map/all_gather | solution.py:85
  1242.7 222.7 %all-gather.13.cloned.1.call-done = bf16[2048,2048]{1,0:T(8,128)(2,1)} async-done(((bf16[2048,128]{1,0:T(8,128)(2,1)}), bf16[2048,2048]{1,0:T(8,128)(2,1)}) %all-gather.13.cloned.1.call-update) | async-done | bytes 8388624 | tf_op jit(solution)/shard_map/all_gather | solution.py:88
  1465.3 5.1 multiply_reduce_fusion.1
  1470.4 1.4 gather_fusion
  1471.8 1.6 convert_select_fusion
  1473.3 107.9 %all-reduce.1 = bf16[256,2048]{1,0:T(8,128)(2,1)S(1)} all-reduce(f32[256,2048]{1,0:T(8,128)} %convert_select_fusion), channel_id=1, replica_groups=mesh['dp'=16,'feat'=32] {'dp','feat'}, use_global_device_ids=true, to_apply=%region_4.5 | all-reduce | flops 524288 | bytes 3145728 | tf_op jit(solution)/shard_map/psum | solution.py:92
  1581.5 0.5 fusion.2
  1582.0 0.5 multiply_minimum_fusion
  (26 shorter events, 0.8 us)
Async XLA Ops:
  6.5 1458.8 %copy-start = (bf16[64,2048]{1,0:T(8,128)(2,1)S(1)}, bf16[64,2048]{1,0:T(8,128)(2,1)}, u32[]{:S(2)}) copy-start(bf16[64,2048]{1,0:T(8,128)(2,1)} %param.5) | copy-start | bytes 786436
  6.5 76.8 %all-gather.7.cloned.1.call-start = ((), (), s32[]{:S(2)}) async-start(), calls=%async_computation.1 | async-start | bytes 4325376 | tf_op jit(solution)/shard_map/all_gather | solution.py:57
  7.3 883.1 %all-gather.15.cloned.1.call-start = ((), (), s32[]{:S(2)}) async-start(), calls=%async_computation.6 | async-start | bytes 4202496 | tf_op jit(solution)/shard_map/all_gather | solution.py:11
  8.9 996.3 %reduce-scatter.2.cloned.1.call-start = ((), (), s32[]{:S(2)}) async-start(), calls=%async_computation.2 | async-start | bytes 557056 | tf_op jit(solution)/shard_map/reduce_scatter | solution.py:63
  87.4 982.0 %all-gather.9.cloned.1.call-start = ((), (), s32[]{:S(2)}) async-start(), calls=%async_computation.3 | async-start | bytes 1081344 | tf_op jit(solution)/shard_map/all_gather | solution.py:66
  897.7 344.9 %copy-start.1 = (s32[256]{0:T(256)S(1)}, s32[256]{0:T(256)}, u32[]{:S(2)}) copy-start(s32[256]{0:T(256)} %param.7) | copy-start | bytes 3076
  1006.6 128.2 %all-gather.11.cloned.1.call-start = ((), (), s32[]{:S(2)}) async-start(), calls=%async_computation.4 | async-start | bytes 1081344 | tf_op jit(solution)/shard_map/all_gather | solution.py:78
  1072.2 393.1 %all-gather.13.cloned.1.call-start = ((), (), s32[]{:S(2)}) async-start(), calls=%async_computation.5 | async-start | bytes 8912896 | tf_op jit(solution)/shard_map/all_gather | solution.py:88
  1471.8 110.3 %copy-start.2 = (f32[64]{0:T(128)S(1)}, f32[64]{0:T(128)}, u32[]{:S(2)}) copy-start(f32[64]{0:T(128)} %param.6) | copy-start | bytes 772
Sparse Core Ops, SparseCore 0:
  9.5 73.7 all-gather.6
  85.5 804.7 all-gather.14
  894.4 110.6 reduce-scatter.1
  1007.4 62.0 all-gather.8
  1072.4 62.4 all-gather.10
  1242.7 222.5 all-gather.12

commit v2 on v0

--- a/solution.py
+++ b/solution.py
@@ -5,6 +5,12 @@
 
 EPSILON = 1e-06
 HIGHEST = lax.Precision.HIGHEST
+measure_scenes_in = lambda piece_in: jnp.concatenate(
+    lax.all_to_all(
+        jnp.stack([piece_in for _ in range(lax.axis_size("feat"))], axis=0), "feat", 0, 0
+    ),
+    axis=0,
+)
 
 
 def contract_rows(left_part, right_part):
@@ -69,9 +75,7 @@
     first_cols = 0.5 * (3.0 * eye_cols - corr_cols)
     updated_y = jnp.dot(corr_rows, first_cols, precision=HIGHEST)
     left_part = first_rows
-    middle = jnp.dot(
-        left_part, lax.all_gather(updated_y, "feat", axis=0, tiled=True), precision=HIGHEST
-    )
+    middle = jnp.dot(left_part, measure_scenes_in(updated_y), precision=HIGHEST)
     second_factor = 0.5 * (3.0 * eye_block - middle)
     root_block = jnp.dot(
         lax.all_gather(second_factor, "dp", axis=1, tiled=True), first_cols, precision=HIGHEST

time: 782 us -> 748 us (0.957)
  waiting for transfers between devices: 375 us -> 342 us
    all_gather x1 -> x0, waiting for transfers between devices: 62.7 us -> none  [per_device(): lax.all_gather(updated_y, 'feat', axis=0, tiled=True)]
    all_to_all x0 -> x1, waiting for transfers between devices: none -> 27.8 us  [lax.all_to_all(jnp.stack([piece_in for _ in range(lax.axis_size('feat'))]...]
where the time goes in v2:
time: 748 us
  blocking collectives  366 us (49%)
  waiting for transfers between devices  342 us (46%)
  matrix products  13.7 us (2%)
  between operations  13.3 us (2%)
    all_gather x1, waiting for transfers between devices, per_device(): lax.all_gather(weight_cols, 'dp', axis=1, tiled=True)  223 us
    psum x1, blocking collectives, per_device(): centre_full = lax.psum(contribution, ('dp', 'feat')).astype(jnp.bfloat16)  108 us
    psum x1, blocking collectives, per_device(): col_squares = lax.psum(own_squares, ('dp', 'feat'))  106 us
    all_gather x1, waiting for transfers between devices, per_device(): portion = lax.all_gather(sample, 'feat', axis=0, tiled=True)  76 us
    all_gather x1, blocking collectives, per_device(): corr_rows = lax.all_gather(corr_block, 'dp', axis=1, tiled=True)  51.8 us
    all_gather x1, blocking collectives, per_device(): lax.all_gather(second_factor, 'dp', axis=1, tiled=True)  50.1 us
    all_gather x1, blocking collectives, per_device(): weight_cols = lax.all_gather(weight_block, 'feat', axis=0, tiled=True)  50.1 us
    all_to_all x1, waiting for transfers between devices, lax.all_to_all(jnp.stack([piece_in for _ in range(lax.axis_size('feat'))]...  27.8 us
  transfers between devices with their start and end apart: 5, of which 5 were waited for; matrix products, arithmetic and copies ran while one was open for 0% of the time, Pallas kernels for 0%

profile of v2, /device:TPU:1, one launch (start us, length us, event | category | flops | bytes accessed | tf_op | source)
XLA Modules:
  0.0 747.7 jit_solution(14212397018333000163)
XLA Ops:
  6.5 0.7 all-gather.4.cloned.1.call-update
  7.3 76.0 %all-gather.4.cloned.1.call-done = bf16[1024,2048]{1,0:T(8,128)(2,1)} async-done(((bf16[32,2048]{1,0:T(8,128)(2,1)}), bf16[1024,2048]{1,0:T(8,128)(2,1)}) %all-gather.4.cloned.1.call-update) | async-done | bytes 4194320 | tf_op jit(solution)/shard_map/all_gather | solution.py:58
  83.3 4.0 convolution_multiply_fusion
  87.5 105.6 %psum.14 = f32[2048]{0:T(1024)S(1)} all-reduce(f32[2048]{0:T(1024)S(1)} %multiply_reduce_fusion.2), channel_id=1, replica_groups=mesh['dp'=16,'feat'=32] {'dp','feat'}, use_global_device_ids=true, to_apply=%region_1.0 | all-reduce | flops 2048 | bytes 16384 | tf_op jit(solution)/shard_map/psum | solution.py:56
  193.2 3.4 reduce-scatter.2.cloned.1.call-done
  196.6 1.4 multiply_multiply_fusion
  198.1 51.8 %all_gather.19 = f32[64,2048]{1,0:T(8,128)S(1)} all-gather(f32[64,128]{1,0:T(8,128)} %multiply_multiply_fusion), channel_id=1, replica_groups=mesh['dp'=16,'feat'=32] {'dp'}, dimensions={1}, use_global_device_ids=true | all-gather | bytes 557056 | tf_op jit(solution)/shard_map/all_gather | solution.py:66
  249.9 11.3 %all-gather.6.cloned.1.call-done = f32[2048,128]{1,0:T(8,128)} async-done(((f32[64,128]{1,0:T(8,128)}), f32[2048,128]{1,0:T(8,128)}) %all-gather.6.cloned.1.call-update) | async-done | bytes 1048592 | tf_op jit(solution)/shard_map/all_gather | solution.py:67
  261.2 2.2 fusion.5
  263.4 1.2 stack.2
  264.6 6.3 all-to-all-start
  271.0 27.8 %all-to-all-done = f32[32,64,128]{2,1,0:T(8,128)S(1)} async-done(((f32[32,64,128]{2,1,0:T(8,128)}), f32[32,64,128]{2,1,0:T(8,128)S(1)}, u32[]{:S(2)}, u32[]{:S(2)}) %all-to-all-start) | async-done | bytes 1048608 | tf_op jit(solution)/shard_map/all_to_all | solution.py:9
  298.8 0.9 fusion.3
  299.7 50.1 %all_gather.21 = f32[64,2048]{1,0:T(8,128)S(1)} all-gather(f32[64,128]{1,0:T(8,128)S(1)} %fusion.3), channel_id=1, replica_groups=mesh['dp'=16,'feat'=32] {'dp'}, dimensions={1}, use_global_device_ids=true | all-gather | bytes 557056 | tf_op jit(solution)/shard_map/all_gather | solution.py:81
  349.8 0.9 fusion.4
  350.7 50.1 %all_gather.22 = bf16[2048,128]{1,0:T(8,128)(2,1)} all-gather(bf16[64,128]{1,0:T(8,128)(2,1)S(1)} %fusion.4), channel_id=1, replica_groups=mesh['dp'=16,'feat'=32] {'feat'}, dimensions={0}, use_global_device_ids=true | all-gather | bytes 540672 | tf_op jit(solution)/shard_map/all_gather | solution.py:84
  400.9 222.9 %all-gather.8.cloned.1.call-done = bf16[2048,2048]{1,0:T(8,128)(2,1)} async-done(((bf16[2048,128]{1,0:T(8,128)(2,1)}), bf16[2048,2048]{1,0:T(8,128)(2,1)}) %all-gather.8.cloned.1.call-update) | async-done | bytes 8388624 | tf_op jit(solution)/shard_map/all_gather | solution.py:87
  623.9 5.1 multiply_reduce_fusion.1
  628.9 1.4 gather_fusion
  630.3 1.6 convert_select_fusion
  631.9 107.9 %all-reduce.1 = bf16[256,2048]{1,0:T(8,128)(2,1)S(1)} all-reduce(f32[256,2048]{1,0:T(8,128)} %convert_select_fusion), channel_id=1, replica_groups=mesh['dp'=16,'feat'=32] {'dp','feat'}, use_global_device_ids=true, to_apply=%region_4.5 | all-reduce | flops 524288 | bytes 3145728 | tf_op jit(solution)/shard_map/psum | solution.py:91
  739.8 0.3 multiply_reduce_fusion
  740.1 0.5 fusion.2
  740.6 0.5 multiply_minimum_fusion
  (26 shorter events, 0.4 us)
Async XLA Ops:
  6.5 617.3 %copy-start = (bf16[64,2048]{1,0:T(8,128)(2,1)S(1)}, bf16[64,2048]{1,0:T(8,128)(2,1)}, u32[]{:S(2)}) copy-start(bf16[64,2048]{1,0:T(8,128)(2,1)} %param.5) | copy-start | bytes 786436
  6.5 80.9 %copy-start.2 = (bf16[32,2048]{1,0:T(8,128)(2,1)S(1)}, bf16[32,2048]{1,0:T(8,128)(2,1)}, u32[]{:S(2)}) copy-start(bf16[32,2048]{1,0:T(8,128)(2,1)} %param.4) | copy-start | bytes 393220
  6.5 76.8 %all-gather.4.cloned.1.call-start = ((), (), s32[]{:S(2)}) async-start(), calls=%async_computation.2 | async-start | bytes 4325376 | tf_op jit(solution)/shard_map/all_gather | solution.py:58
  7.3 189.4 %reduce-scatter.2.cloned.1.call-start = ((), (), s32[]{:S(2)}) async-start(), calls=%async_computation.3 | async-start | bytes 557056 | tf_op jit(solution)/shard_map/reduce_scatter | solution.py:64
  87.4 173.8 %all-gather.6.cloned.1.call-start = ((), (), s32[]{:S(2)}) async-start(), calls=%async_computation.4 | async-start | bytes 1081344 | tf_op jit(solution)/shard_map/all_gather | solution.py:67
  261.2 88.6 %copy-start.1 = (f32[2048,128]{1,0:T(8,128)S(1)}, f32[2048,128]{1,0:T(8,128)}, u32[]{:S(2)}) copy-start(f32[2048,128]{1,0:T(8,128)} %all-gather.6.cloned.1.call-done) | copy-start | bytes 3145732
  263.4 137.4 %copy-start.3 = (s32[256]{0:T(256)S(1)}, s32[256]{0:T(256)}, u32[]{:S(2)}) copy-start(s32[256]{0:T(256)} %param.7) | copy-start | bytes 3076
  264.6 34.2 %all-to-all-start = ((f32[32,64,128]{2,1,0:T(8,128)}), f32[32,64,128]{2,1,0:T(8,128)S(1)}, u32[]{:S(2)}, u32[]{:S(2)}) async-start(f32[32,64,128]{2,1,0:T(8,128)} %stack.2), calls=%async_computation.1 | async-start | bytes 2097152 | tf_op jit(solution)/shard_map/all_to_all | solution.py:9
  270.9 353.0 %all-gather.8.cloned.1.call-start = ((), (), s32[]{:S(2)}) async-start(), calls=%async_computation.5 | async-start | bytes 8912896 | tf_op jit(solution)/shard_map/all_gather | solution.py:87
  630.3 110.3 %copy-start.4 = (f32[64]{0:T(128)S(1)}, f32[64]{0:T(128)}, u32[]{:S(2)}) copy-start(f32[64]{0:T(128)} %param.6) | copy-start | bytes 772
Sparse Core Ops, SparseCore 0:
  9.5 73.7 all-gather.3
  87.5 109.0 reduce-scatter.1
  199.0 62.1 all-gather.5
  401.0 222.8 all-gather.7
